TPU v7x, 128 devices: a whole 4x4x4 slice. The times are simulated.
128 devices in a mesh: samp: 16 (over z_hi, x, core), par: 8 (over y, z_lo).
Axes of the slice: x: 4, y: 4, z: 4 (z_hi: 2, z_lo: 2; z = z_hi * 2 + z_lo), core: 2. Of those that a mesh axis runs over, the one named last changes fastest.
Arguments:
- activations: bfloat16 [10240, 2048], P('samp', 'par'), may hold values from -128 to 128
- signal: bfloat16 [10240, 2], P('samp'), may hold values from -40 to 40
Outputs:
- gram: float32 [10240, 10240], P('samp', 'par')
- panels: float32 [10240, 1280], P('samp', 'par')
All inputs are finite; a program needn't handle non-finite values.
Results may differ from a plain program's by a relative error of at most 0.0022.
Values may be sent and summed in bfloat16 or wider, within the bound.
A program may use at most 128 MiB of HBM per device.

v0:
```python
import jax
import jax.numpy as jnp
from jax import lax
from jax.sharding import PartitionSpec as P

DAMPING = 0.5
EPSILON = 1e-05


def from_root(value, axis, root):
    mine = lax.axis_index(axis) == root
    return lax.psum(jnp.where(mine, value, jnp.zeros_like(value)), axis)


def right_solve(factor, block):
    return jax.scipy.linalg.solve_triangular(factor, block.T, lower=True).T


def first_moment(signal, active):
    return jnp.dot(signal.T, active, preferred_element_type=jnp.float32)


def second_moment(signal_float, active_float):
    products = signal_float[:, :, None] * active_float[:, None, :]
    return jnp.sum(products * products, axis=0)


def normalize(moment_one, moment_two, sample_total, slab_width):
    average = moment_one / sample_total
    column_scale = 1.0 / jnp.sqrt(
        slab_width * (moment_two / sample_total - average * average + EPSILON)
    )
    return (average, column_scale)


def build_rows(signal_float, active_float, average, column_scale):
    centered = signal_float[:, :, None] * active_float[:, None, :] - average[None]
    return (centered * column_scale[None]).astype(jnp.bfloat16)


def per_device(activations, signal):
    signal_float = signal.astype(jnp.float32)
    local_count = activations.shape[0]
    samp_count = lax.axis_size("samp")
    par_count = lax.axis_size("par")
    sample_total = local_count * samp_count
    slab_width = signal.shape[1] * activations.shape[1] * par_count
    active_float = activations.astype(jnp.float32)
    sum_one = first_moment(signal, activations)
    sum_two = second_moment(signal_float, active_float)
    moment_one, moment_two = lax.psum((sum_one, sum_two), "samp")
    average, column_scale = normalize(moment_one, moment_two, sample_total, slab_width)
    local_rows = build_rows(signal_float, active_float, average, column_scale)
    full_rows = lax.all_gather(local_rows, "par", axis=2, tiled=True).reshape(
        local_count, slab_width
    )
    blocks_per = samp_count // par_count
    column = lax.axis_index("par")
    samp_index = lax.axis_index("samp")
    pieces = []
    for offset in range(blocks_per):
        partner = from_root(full_rows, "samp", column * blocks_per + offset)
        pieces.append(
            lax.dot_general(
                full_rows, partner, (((1,), (1,)), ((), ())), preferred_element_type=jnp.float32
            )
        )
    gram_tile = jnp.concatenate(pieces, axis=1)
    global_row = samp_index * local_count + lax.broadcasted_iota(jnp.int32, gram_tile.shape, 0)
    global_col = column * (blocks_per * local_count) + lax.broadcasted_iota(
        jnp.int32, gram_tile.shape, 1
    )
    gram_tile = gram_tile + jnp.where(
        global_row == global_col, jnp.float32(DAMPING), jnp.float32(0.0)
    )
    column_block = from_root(gram_tile, "par", 0)
    identity = jnp.eye(local_count, dtype=jnp.float32)
    first_cols = column_block[:, :local_count]
    second_cols = column_block[:, local_count:]
    factor_one = jnp.linalg.cholesky(jnp.where(samp_index == 0, first_cols, identity))
    factor_one = from_root(factor_one, "samp", 0)
    panel_one = right_solve(factor_one, first_cols)
    partner_panel = from_root(panel_one, "samp", 1)
    update = second_cols - jnp.dot(panel_one, partner_panel.T, precision=lax.Precision.HIGHEST)
    factor_two = jnp.linalg.cholesky(jnp.where(samp_index == 1, update, identity))
    factor_two = from_root(factor_two, "samp", 1)
    panel_two = right_solve(factor_two, update)
    panel_two = jnp.where(samp_index == 0, jnp.float32(0.0), panel_two)
    both_panels = jnp.concatenate([panel_one, panel_two], axis=1)
    own_width = both_panels.shape[1] // par_count
    own_panels = lax.dynamic_slice_in_dim(both_panels, column * own_width, own_width, 1)
    return (gram_tile, own_panels)


def solution(mesh):
    in_specs = (P("samp", "par"), P("samp", None))
    out_specs = (P("samp", "par"), P("samp", "par"))
    return jax.shard_map(
        per_device, mesh=mesh, in_specs=in_specs, out_specs=out_specs, check_vma=False
    )
```

profile of v0, /device:TPU:1, one launch (start us, length us, event | category | flops | bytes accessed | tf_op | source)
XLA Modules:
  0.0 1360.1 jit_solution(4430709151654853441)
XLA Ops:
  10.4 34.8 %all-reduce.1 = (f32[2,256]{1,0:T(2,128)S(1)}, f32[2,256]{1,0:T(2,128)S(1)}) all-reduce(f32[2,256]{1,0:T(2,128)S(1)} %fusion.8, f32[2,256]{1,0:T(2,128)S(1)} %fusion.104), channel_id=1, replica_groups=mesh['samp'=16,'par'=8] {'samp'}, use_global_device_ids=true, to_apply=%region_2.0 | all-reduce | flops 1024 | bytes 8192 | tf_op jit(solution)/shard_map/psum | solution.py:51
  46.4 110.9 %all-gather.2.cloned.1.call-done = bf16[640,2,2048]{0,2,1:T(8,128)(2,1)} async-done(((bf16[640,2,256]{0,2,1:T(8,128)(2,1)}), bf16[640,2,2048]{0,2,1:T(8,128)(2,1)}) %all-gather.2.cloned.1.call-update) | async-done | bytes 5242896 | tf_op jit(solution)/shard_map/all_gather | solution.py:54
  157.3 7.3 broadcast_select_fusion.1
  164.7 169.7 %all-reduce.17.cloned.1.call-done = (bf16[640,4096]{0,1:T(8,128)(2,1)}, bf16[640,4096]{0,1:T(8,128)(2,1)}) async-done(((bf16[640,4096]{0,1:T(8,128)(2,1)}, bf16[640,4096]{0,1:T(8,128)(2,1)}), (bf16[640,4096]{0,1:T(8,128)(2,1)}, bf16[640,4096]{0,1:T(8,128)(2,1)})) %all-reduce.17.cloned.1.call-update) | async-done | bytes 10485776 | tf_op jit(solution)/shard_map/psum | solution.py:12
  334.4 8.6 fusion.105
  343.1 4.5 fusion.106
  347.6 3.3 broadcast_select_fusion.2
  351.0 149.1 %all-reduce.9.cloned.1.call-done = f32[640,1280]{0,1:T(8,128)} async-done(((f32[640,1280]{0,1:T(8,128)}), f32[640,1280]{0,1:T(8,128)}) %all-reduce.9.cloned.1.call-update) | async-done | bytes 3276816 | tf_op jit(solution)/shard_map/psum | solution.py:12
  500.2 2.8 convert_select_fusion.1
  505.8 11.7 cholesky.364
  517.7 9.8 custom-call.34
  528.9 13.2 cholesky.383
  543.5 11.4 custom-call.35
  556.6 12.3 cholesky.404
  570.5 10.4 custom-call.36
  582.5 11.9 cholesky.423
  595.2 9.8 custom-call.37
  605.6 11.7 cholesky.440
  623.2 144.2 %all-reduce.11.cloned.1.call-done = f32[640,640]{1,0:T(8,128)} async-done(((f32[640,640]{1,0:T(8,128)}), f32[640,640]{1,0:T(8,128)}) %all-reduce.11.cloned.1.call-update) | async-done | bytes 1638416 | tf_op jit(solution)/shard_map/psum | solution.py:12
  769.8 13.5 while.4
  770.8 2.0 bitcast_dynamic-update-slice_fusion.4
  773.5 2.0 bitcast_dynamic-update-slice_fusion.4
  776.1 2.0 bitcast_dynamic-update-slice_fusion.4
  778.7 2.0 bitcast_dynamic-update-slice_fusion.4
  781.3 2.0 bitcast_dynamic-update-slice_fusion.4
  783.3 50.6 %custom-call.38 = f32[5,128,128]{1,2,0:T(8,128)} custom-call(f32[5,128,128]{2,1,0:T(8,128)} %get-tuple-element.18), custom_call_target="InvertDiagBlocksLowerTriangular" | custom-call | tf_op jit(solution)/shard_map/jit(_solve_triangular)/triangular_solve | solution.py:16
  841.3 2.6 fusion.28
  848.4 144.0 %all-reduce.13.cloned.1.call-done = f32[640,640]{1,0:T(8,128)} async-done(((f32[640,640]{1,0:T(8,128)}), f32[640,640]{1,0:T(8,128)}) %all-reduce.13.cloned.1.call-update) | async-done | bytes 1638416 | tf_op jit(solution)/shard_map/psum | solution.py:12
  992.4 7.7 convert_select_fusion
  1004.7 11.7 cholesky.455
  1016.5 9.8 custom-call.39
  1029.6 13.2 cholesky.474
  1045.7 11.5 custom-call.40
  1059.7 12.3 cholesky.495
  1073.6 10.4 custom-call.41
  1086.5 12.1 cholesky.514
  1099.3 9.8 custom-call.42
  1110.5 11.7 cholesky.531
  1127.4 4.6 copy.59
  1132.0 139.5 %all-reduce.15.cloned.1.call-done = f32[640,640]{1,0:T(8,128)} async-done(((f32[640,640]{1,0:T(8,128)}), f32[640,640]{1,0:T(8,128)}) %all-reduce.15.cloned.1.call-update) | async-done | bytes 1638416 | tf_op jit(solution)/shard_map/psum | solution.py:12
  1273.7 13.2 while.5
  1274.4 2.0 bitcast_dynamic-update-slice_fusion.5
  1277.0 2.0 bitcast_dynamic-update-slice_fusion.5
  1279.7 2.0 bitcast_dynamic-update-slice_fusion.5
  1282.3 2.0 bitcast_dynamic-update-slice_fusion.5
  1285.0 2.0 bitcast_dynamic-update-slice_fusion.5
  1287.0 50.8 %custom-call.43 = f32[5,128,128]{1,2,0:T(8,128)} custom-call(f32[5,128,128]{2,1,0:T(8,128)} %get-tuple-element.19), custom_call_target="InvertDiagBlocksLowerTriangular" | custom-call | tf_op jit(solution)/shard_map/jit(_solve_triangular)/triangular_solve | solution.py:16
  1345.7 2.7 fusion.25
  (160 shorter events, 76.2 us)
Async XLA Ops:
  7.2 150.1 %all-gather.2.cloned.1.call-start = ((), (), s32[]{:S(2)}) async-start(), calls=%async_computation | async-start | bytes 5898240 | tf_op jit(solution)/shard_map/all_gather | solution.py:54
  46.4 288.1 %all-reduce.17.cloned.1.call-start = ((), (), s32[]{:S(2)}) async-start(), calls=%async_computation.5 | async-start | bytes 20971520 | tf_op jit(solution)/shard_map/psum | solution.py:12
  164.6 178.5 %slice-start = ((s8[5242880]{0:T(1024)(128)(4,1)}), s8[1048576]{0:T(1024)(128)(4,1)S(1)}, s32[]{:S(2)}) async-start(s8[5242880]{0:T(1024)(128)(4,1)} %bitcast.139), calls=%async_computation.6 | async-start | bytes 2097152
  164.6 335.5 %all-reduce.9.cloned.1.call-start = ((), (), s32[]{:S(2)}) async-start(), calls=%async_computation.1 | async-start | bytes 6553600 | tf_op jit(solution)/shard_map/psum | solution.py:12
  334.4 8.6 slice-start.1
  334.4 8.7 copy-start.10
  351.0 416.5 %all-reduce.11.cloned.1.call-start = ((), (), s32[]{:S(2)}) async-start(), calls=%async_computation.2 | async-start | bytes 3276800 | tf_op jit(solution)/shard_map/psum | solution.py:12
  504.6 1.2 copy-start.2
  505.8 21.7 %copy-start.3 = (f32[640,640]{1,0:T(8,128)S(1)}, f32[640,640]{1,0:T(8,128)}, u32[]{:S(2)}) copy-start(f32[640,640]{1,0:T(8,128)} %copy-done.2) | copy-start | bytes 4915204
  623.2 369.2 %all-reduce.13.cloned.1.call-start = ((), (), s32[]{:S(2)}) async-start(), calls=%async_computation.3 | async-start | bytes 3276800 | tf_op jit(solution)/shard_map/psum | solution.py:12
  623.2 210.7 %copy-start = (f32[640,640]{1,0:T(8,128)S(1)}, f32[640,640]{1,0:T(8,128)}, u32[]{:S(2)}) copy-start(f32[640,640]{1,0:T(8,128)} %get-tuple-element.55) | copy-start | bytes 4915204
  783.3 50.6 %copy-start.5 = (f32[640,640]{1,0:T(8,128)}, f32[640,640]{1,0:T(8,128)S(1)}, u32[]{:S(2)}) copy-start(f32[640,640]{1,0:T(8,128)S(1)} %get-tuple-element.202) | copy-start | bytes 4915204
  833.9 2.7 copy-start.8
  844.5 1.0 copy-start.6
  848.4 423.1 %all-reduce.15.cloned.1.call-start = ((), (), s32[]{:S(2)}) async-start(), calls=%async_computation.4 | async-start | bytes 3276800 | tf_op jit(solution)/shard_map/psum | solution.py:12
  1003.5 1.2 copy-start.1
  1286.9 50.8 %copy-start.4 = (f32[640,640]{1,0:T(8,128)}, f32[640,640]{1,0:T(8,128)S(1)}, u32[]{:S(2)}) copy-start(f32[640,640]{1,0:T(8,128)S(1)} %get-tuple-element.201) | copy-start | bytes 4915204
  1337.7 3.0 copy-start.9
  1349.1 1.0 copy-start.7
Sparse Core Ops, SparseCore 0:
  46.5 110.7 all-gather.1
  164.8 169.6 all-reduce.16
  351.1 149.0 all-reduce.8
  623.3 144.1 all-reduce.10
  848.5 143.8 all-reduce.12
  1127.5 143.8 all-reduce.14
where the time goes:
time: 1370 us; the launch traced here: 1360 us
  waiting for transfers between devices  858 us (63%)
  other arithmetic  342 us (25%)
  matrix products  59.1 us (4%)
  local copies, waits for them, and re-layouts  44.9 us (3%)
  blocking collectives  34.8 us (3%)
  between operations  21.2 us (2%)
    psum x5, waiting for transfers between devices, from_root(): return lax.psum(jnp.where(mine, value, jnp.zeros_like(value)), axis)  747 us
    all_gather x1, waiting for transfers between devices, per_device(): lax.all_gather(local_rows, 'par', axis=2, tiled=True)  111 us
    another operation x19, other arithmetic, per_device(): jnp.linalg.cholesky(jnp.where(samp_index == 1, update, identity))  108 us
    another operation x18, other arithmetic, per_device(): jnp.linalg.cholesky(jnp.where(samp_index == 0, first_cols, identity))  107 us
    another operation x5, other arithmetic, right_solve(): return jax.scipy.linalg.solve_triangular(factor, block.T, lower=True).T  104 us
    psum x1, blocking collectives, per_device(): moment_one, moment_two = lax.psum((sum_one, sum_two), 'samp')  34.8 us
    another operation x41, local copies, waits for them, and re-layouts, right_solve(): return jax.scipy.linalg.solve_triangular(factor, block.T, lower=True).T  29.2 us
  transfers between devices with their start and end apart: 6, of which 6 were waited for; matrix products, arithmetic and copies ran while one was open for 0% of the time, Pallas kernels for 0%

commit v1 on v0

--- a/solution.py
+++ b/solution.py
@@ -51,9 +51,9 @@
     moment_one, moment_two = lax.psum((sum_one, sum_two), "samp")
     average, column_scale = normalize(moment_one, moment_two, sample_total, slab_width)
     local_rows = build_rows(signal_float, active_float, average, column_scale)
-    full_rows = lax.all_gather(local_rows, "par", axis=2, tiled=True).reshape(
-        local_count, slab_width
-    )
+    full_rows = jnp.concatenate(
+        lax.all_to_all(jnp.stack([local_rows] * lax.axis_size("par")), "par", 0, 0), axis=2
+    ).reshape(local_count, slab_width)
     blocks_per = samp_count // par_count
     column = lax.axis_index("par")
     samp_index = lax.axis_index("samp")

time: 1370 us -> 1330 us (0.971)
  waiting for transfers between devices: 858 us -> 816 us
    all_gather x1 -> x0, waiting for transfers between devices: 111 us -> none  [per_device(): lax.all_gather(local_rows, 'par', axis=2, tiled=True)]
    all_to_all x0 -> x1, waiting for transfers between devices: none -> 70.9 us  [per_device(): lax.all_to_all(jnp.stack([local_rows] * lax.axis_size('par')), 'par', 0, 0)]
where the time goes in v1:
time: 1330 us; the launch traced here: 1320 us
  waiting for transfers between devices  816 us (61%)
  other arithmetic  339 us (25%)
  matrix products  57.5 us (4%)
  local copies, waits for them, and re-layouts  50 us (4%)
  blocking collectives  34.8 us (3%)
  between operations  20.9 us (2%)
    psum x5, waiting for transfers between devices, from_root(): return lax.psum(jnp.where(mine, value, jnp.zeros_like(value)), axis)  745 us
    another operation x19, other arithmetic, per_device(): jnp.linalg.cholesky(jnp.where(samp_index == 1, update, identity))  108 us
    another operation x18, other arithmetic, per_device(): jnp.linalg.cholesky(jnp.where(samp_index == 0, first_cols, identity))  107 us
    another operation x5, other arithmetic, right_solve(): return jax.scipy.linalg.solve_triangular(factor, block.T, lower=True).T  104 us
    all_to_all x1, waiting for transfers between devices, per_device(): lax.all_to_all(jnp.stack([local_rows] * lax.axis_size('par')), 'par', 0, 0)  70.9 us
    psum x1, blocking collectives, per_device(): moment_one, moment_two = lax.psum((sum_one, sum_two), 'samp')  34.8 us
    another operation x41, local copies, waits for them, and re-layouts, right_solve(): return jax.scipy.linalg.solve_triangular(factor, block.T, lower=True).T  29.1 us
  transfers between devices with their start and end apart: 6, of which 6 were waited for; matrix products, arithmetic and copies ran while one was open for 0% of the time, Pallas kernels for 0%

profile of v1, /device:TPU:1, one launch (start us, length us, event | category | flops | bytes accessed | tf_op | source)
XLA Modules:
  0.0 1324.2 jit_solution(14180577896767023048)
XLA Ops:
  10.4 34.8 %all-reduce.1 = (f32[2,256]{1,0:T(2,128)S(1)}, f32[2,256]{1,0:T(2,128)S(1)}) all-reduce(f32[2,256]{1,0:T(2,128)S(1)} %fusion.8, f32[2,256]{1,0:T(2,128)S(1)} %fusion.104), channel_id=1, replica_groups=mesh['samp'=16,'par'=8] {'samp'}, use_global_device_ids=true, to_apply=%region_2.0 | all-reduce | flops 1024 | bytes 8192 | tf_op jit(solution)/shard_map/psum | solution.py:51
  45.5 3.0 stack.2
  48.4 4.7 all-to-all-start
  53.2 70.9 %all-to-all-done = bf16[8,640,2,256]{1,3,2,0:T(8,128)(2,1)} async-done(((bf16[8,640,2,256]{1,3,2,0:T(8,128)(2,1)}), bf16[8,640,2,256]{1,3,2,0:T(8,128)(2,1)}, u32[]{:S(2)}, u32[]{:S(2)}) %all-to-all-start) | async-done | bytes 5242912 | tf_op jit(solution)/shard_map/all_to_all | solution.py:55
  124.1 2.9 copy.43
  127.1 5.6 broadcast_select_fusion.1
  133.1 168.3 %all-reduce.17.cloned.1.call-done = (bf16[640,4096]{0,1:T(8,128)(2,1)}, bf16[640,4096]{0,1:T(8,128)(2,1)}) async-done(((bf16[640,4096]{0,1:T(8,128)(2,1)}, bf16[640,4096]{0,1:T(8,128)(2,1)}), (bf16[640,4096]{0,1:T(8,128)(2,1)}, bf16[640,4096]{0,1:T(8,128)(2,1)})) %all-reduce.17.cloned.1.call-update) | async-done | bytes 10485776 | tf_op jit(solution)/shard_map/psum | solution.py:12
  301.4 8.6 fusion.105
  310.1 4.5 fusion.106
  314.6 3.3 broadcast_select_fusion.2
  318.0 149.1 %all-reduce.9.cloned.1.call-done = f32[640,1280]{0,1:T(8,128)} async-done(((f32[640,1280]{0,1:T(8,128)}), f32[640,1280]{0,1:T(8,128)}) %all-reduce.9.cloned.1.call-update) | async-done | bytes 3276816 | tf_op jit(solution)/shard_map/psum | solution.py:12
  467.1 2.8 convert_select_fusion.1
  472.9 11.7 cholesky.364
  484.7 9.8 custom-call.34
  495.9 13.2 cholesky.383
  510.6 11.4 custom-call.35
  523.6 12.3 cholesky.404
  537.5 10.4 custom-call.36
  549.6 11.9 cholesky.423
  562.2 9.8 custom-call.37
  572.6 11.7 cholesky.440
  590.2 144.2 %all-reduce.11.cloned.1.call-done = f32[640,640]{1,0:T(8,128)} async-done(((f32[640,640]{1,0:T(8,128)}), f32[640,640]{1,0:T(8,128)}) %all-reduce.11.cloned.1.call-update) | async-done | bytes 1638416 | tf_op jit(solution)/shard_map/psum | solution.py:12
  734.4 2.7 fusion.4
  737.2 14.3 %while.4 = (s32[]{:T(128)}, f32[640,640]{1,0:T(8,128)}, s32[5,2]{0,1:T(2,128)S(1)}, f32[5,128,128]{2,1,0:T(8,128)S(1)}, s32[]{:T(128)}) while((s32[]{:T(128)}, f32[640,640]{1,0:T(8,128)}, s32[5,2]{0,1:T(2,128)S(1)}, f32[5,128,128]{2,1,0:T(8,128)S(1)}, s32[]{:T(128)}) %tuple.67), condition=%wide.while_cond, body=%wide.while_body.sunk | while | flops 2 | bytes 131181 | solution.py:16
  738.2 2.2 bitcast_dynamic-update-slice_fusion.4
  741.0 2.2 bitcast_dynamic-update-slice_fusion.4
  743.8 2.2 bitcast_dynamic-update-slice_fusion.4
  746.6 2.2 bitcast_dynamic-update-slice_fusion.4
  749.4 2.1 bitcast_dynamic-update-slice_fusion.4
  751.5 49.1 %custom-call.38 = f32[5,128,128]{1,2,0:T(8,128)S(1)} custom-call(f32[5,128,128]{2,1,0:T(8,128)S(1)} %get-tuple-element.18), custom_call_target="InvertDiagBlocksLowerTriangular" | custom-call | tf_op jit(solution)/shard_map/jit(_solve_triangular)/triangular_solve | solution.py:16
  812.7 144.2 %all-reduce.13.cloned.1.call-done = f32[640,640]{1,0:T(8,128)} async-done(((f32[640,640]{1,0:T(8,128)}), f32[640,640]{1,0:T(8,128)}) %all-reduce.13.cloned.1.call-update) | async-done | bytes 1638416 | tf_op jit(solution)/shard_map/psum | solution.py:12
  956.8 7.7 convert_select_fusion
  969.1 11.7 cholesky.455
  981.0 9.8 custom-call.39
  994.1 13.2 cholesky.474
  1010.1 11.5 custom-call.40
  1024.1 12.3 cholesky.495
  1038.0 10.4 custom-call.41
  1050.9 12.1 cholesky.514
  1063.7 9.8 custom-call.42
  1074.9 11.7 cholesky.531
  1091.8 4.6 copy.60
  1096.4 139.5 %all-reduce.15.cloned.1.call-done = f32[640,640]{1,0:T(8,128)} async-done(((f32[640,640]{1,0:T(8,128)}), f32[640,640]{1,0:T(8,128)}) %all-reduce.15.cloned.1.call-update) | async-done | bytes 1638416 | tf_op jit(solution)/shard_map/psum | solution.py:12
  1238.2 13.2 while.5
  1238.8 2.0 bitcast_dynamic-update-slice_fusion.5
  1249.4 2.0 bitcast_dynamic-update-slice_fusion.5
  1251.4 50.8 %custom-call.43 = f32[5,128,128]{1,2,0:T(8,128)} custom-call(f32[5,128,128]{2,1,0:T(8,128)} %get-tuple-element.19), custom_call_target="InvertDiagBlocksLowerTriangular" | custom-call | tf_op jit(solution)/shard_map/jit(_solve_triangular)/triangular_solve | solution.py:16
  1310.1 2.7 fusion.25
  (159 shorter events, 79.2 us)
Async XLA Ops:
  48.4 75.7 %all-to-all-start = ((bf16[8,640,2,256]{1,3,2,0:T(8,128)(2,1)}), bf16[8,640,2,256]{1,3,2,0:T(8,128)(2,1)}, u32[]{:S(2)}, u32[]{:S(2)}) async-start(bf16[8,640,2,256]{1,3,2,0:T(8,128)(2,1)} %stack.2), calls=%async_computation | async-start | bytes 10485760 | tf_op jit(solution)/shard_map/all_to_all | solution.py:55
  53.1 248.3 %all-reduce.17.cloned.1.call-start = ((), (), s32[]{:S(2)}) async-start(), calls=%async_computation.5 | async-start | bytes 20971520 | tf_op jit(solution)/shard_map/psum | solution.py:12
  127.1 5.6 copy-start
  132.7 177.4 %slice-start = ((s8[5242880]{0:T(1024)(128)(4,1)}), s8[1048576]{0:T(1024)(128)(4,1)S(1)}, s32[]{:S(2)}) async-start(s8[5242880]{0:T(1024)(128)(4,1)} %bitcast.135), calls=%async_computation.6 | async-start | bytes 2097152
  132.7 334.4 %all-reduce.9.cloned.1.call-start = ((), (), s32[]{:S(2)}) async-start(), calls=%async_computation.1 | async-start | bytes 6553600 | tf_op jit(solution)/shard_map/psum | solution.py:12
  301.4 8.6 slice-start.1
  301.4 8.7 copy-start.9
  317.9 416.5 %all-reduce.11.cloned.1.call-start = ((), (), s32[]{:S(2)}) async-start(), calls=%async_computation.2 | async-start | bytes 3276800 | tf_op jit(solution)/shard_map/psum | solution.py:12
  471.7 1.2 copy-start.3
  472.9 21.7 %copy-start.4 = (f32[640,640]{1,0:T(8,128)S(1)}, f32[640,640]{1,0:T(8,128)}, u32[]{:S(2)}) copy-start(f32[640,640]{1,0:T(8,128)} %copy-done.3) | copy-start | bytes 4915204
  590.1 366.7 %all-reduce.13.cloned.1.call-start = ((), (), s32[]{:S(2)}) async-start(), calls=%async_computation.3 | async-start | bytes 3276800 | tf_op jit(solution)/shard_map/psum | solution.py:12
  590.2 210.5 %copy-start.1 = (f32[640,640]{1,0:T(8,128)S(1)}, f32[640,640]{1,0:T(8,128)}, u32[]{:S(2)}) copy-start(f32[640,640]{1,0:T(8,128)} %get-tuple-element.55) | copy-start | bytes 4915204
  800.6 6.0 copy-start.7
  812.6 423.3 %all-reduce.15.cloned.1.call-start = ((), (), s32[]{:S(2)}) async-start(), calls=%async_computation.4 | async-start | bytes 3276800 | tf_op jit(solution)/shard_map/psum | solution.py:12
  967.9 1.2 copy-start.2
  1251.4 50.8 %copy-start.5 = (f32[640,640]{1,0:T(8,128)}, f32[640,640]{1,0:T(8,128)S(1)}, u32[]{:S(2)}) copy-start(f32[640,640]{1,0:T(8,128)S(1)} %get-tuple-element.201) | copy-start | bytes 4915204
  1302.2 3.0 copy-start.8
  1313.5 1.0 copy-start.6
Sparse Core Ops, SparseCore 0:
  132.8 168.5 all-reduce.16
  318.1 149.0 all-reduce.8
  590.2 144.1 all-reduce.10
  812.7 144.0 all-reduce.12
  1091.9 143.8 all-reduce.14
